TPU v7x, 32 devices: a whole 2x2x4 slice. The times are simulated.
32 devices in a mesh: frame: 16 (over z, x, core), batch: 2 (over y).
Axes of the slice: x: 2, y: 2, z: 4, core: 2. Of those that a mesh axis runs over, the one named last changes fastest.
Arguments:
- latents: bfloat16 [32, 256, 640], P(('batch', 'frame')), parts along dimension 0, may hold values from -6 to 6
- query_space: bfloat16 [640, 640], replicated, may hold values from -8 to 8
- key_space: bfloat16 [640, 640], replicated, may hold values from -8 to 8
- value_space: bfloat16 [640, 640], replicated, may hold values from -0.25 to 0.25
- out_space: bfloat16 [640, 640], replicated, may hold values from -0.25 to 0.25
- query_time: bfloat16 [640, 640], replicated, may hold values from -8 to 8
- key_time: bfloat16 [640, 640], replicated, may hold values from -8 to 8
- value_time: bfloat16 [640, 640], replicated, may hold values from -0.25 to 0.25
- out_time: bfloat16 [640, 640], replicated, may hold values from -0.25 to 0.25
- position_bias: float32 [8, 32], replicated, may hold values from -4 to 4
- bucket_table: int32 [257], replicated, may hold values from 0 to 31, as said below
Outputs:
- edited: bfloat16 [32, 256, 640], P(('batch', 'frame')), parts along dimension 0
There are 2 independent parts, one for each index of `batch`. A program takes and returns all parts, laid end to end along the dimension named above; an argument that names none is the same for every part. Nothing has to cross between parts.
Inputs may be any that keep to these rules, and one draw needn't show every extreme that they name: `bucket_table`: entry 128 + d is the bucket of frame offset d; offsets 0 and above take ids below 16, never falling as d grows, offset 0 takes id 0; negative offsets take the other ids, never falling as -d grows.
All inputs are finite; a program needn't handle non-finite values.
Results may differ from a plain program's by a relative error of at most 0.012.
Values may be sent and summed in bfloat16 or wider, within the bound.
A program may use at most 64 MiB of HBM per device.

v0:
```python
import math

import jax
import jax.numpy as jnp
from jax import lax
from jax.sharding import PartitionSpec as P

HEADS = 8
HEAD_DIM = 80


EPS = 1e-05


def from_behind(x, axis, by):
    size = lax.axis_size(axis)
    pairs = [(i, i + by) for i in range(size) if 0 <= i + by < size]
    return lax.ppermute(x, axis, pairs)


def spread_2(block, axis, source):
    block = jnp.where(lax.axis_index(axis) == source, block, jnp.zeros_like(block))
    return lax.psum(block, axis)


def normalize(values):
    floats = values.astype(jnp.float32)
    average = jnp.mean(floats, axis=-1, keepdims=True)
    centred = floats - average
    spread = jnp.mean(centred * centred, axis=-1, keepdims=True)
    return (centred * lax.rsqrt(spread + EPS)).astype(jnp.bfloat16)


def project(rows, weight):
    lead = rows.shape[:-1]
    flat = rows.reshape(-1, rows.shape[-1])
    result = jnp.dot(flat, weight, preferred_element_type=jnp.float32)
    return result.reshape(lead + (weight.shape[1],)).astype(jnp.bfloat16)


def softmax_rows(scores):
    highest = jnp.max(scores, axis=-1, keepdims=True)
    powered = jnp.exp(scores - highest)
    return (powered / jnp.sum(powered, axis=-1, keepdims=True)).astype(jnp.bfloat16)


def temporal_attend(time_q, time_k, time_v, bias_rows):
    frames, places, channels = time_q.shape
    factor = 1.0 / math.sqrt(HEAD_DIM)
    block_rows = math.gcd(frames, 512)
    blocks = frames // block_rows
    limit = (bias_rows.shape[1] - 1) // 2
    key_rows = time_k.reshape(frames, places, HEADS, HEAD_DIM)
    value_rows = time_v.reshape(frames, places, HEADS, HEAD_DIM)
    columns = jnp.arange(frames, dtype=jnp.int32)

    def one_block(begin_row):
        query_rows = time_q.reshape(block_rows, places, HEADS, HEAD_DIM)
        row_ids = begin_row + jnp.arange(block_rows, dtype=jnp.int32)
        offsets = jnp.clip(columns[None, :] - row_ids[:, None], -limit, limit) + limit
        bias = bias_rows[:, offsets]
        scores = (
            jnp.einsum("iphe,jphe->phij", query_rows, key_rows, preferred_element_type=jnp.float32)
            * factor
            + bias[None]
        )
        weights = softmax_rows(scores)
        mixed = jnp.einsum(
            "phij,jphe->iphe", weights, value_rows, preferred_element_type=jnp.float32
        )
        return mixed.astype(jnp.bfloat16).reshape(block_rows, places, channels)

    results = lax.map(one_block, jnp.arange(blocks, dtype=jnp.int32) * block_rows)
    return results.reshape(frames, places, channels)


def squeeze_items(rows):
    return rows.reshape(rows.shape[0], rows.shape[2], rows.shape[3])


def body(
    latents,
    query_space,
    key_space,
    value_space,
    out_space,
    query_time,
    key_time,
    value_time,
    out_time,
    position_bias,
    bucket_table,
):
    frames, places, channels = latents.shape
    factor = 1.0 / math.sqrt(HEAD_DIM)
    normed = normalize(latents)
    space_q = project(normed, query_space)
    space_k = project(normed, key_space)
    space_v = project(normed, value_space)
    prior_pair = from_behind(jnp.stack([space_k[-1], space_v[-1]]), "frame", 1)
    first_pair = spread_2(jnp.stack([space_k[0], space_v[0]]), "frame", 0)
    prior_keys, prior_values = (prior_pair[0], prior_pair[1])
    first_keys, first_values = (first_pair[0], first_pair[1])
    is_first = lax.axis_index("frame") == 0
    prior_keys = jnp.where(is_first, first_keys, prior_keys)
    prior_values = jnp.where(is_first, first_values, prior_values)
    before_keys = jnp.concatenate([prior_keys[None], space_k[:-1]], axis=0)
    before_values = jnp.concatenate([prior_values[None], space_v[:-1]], axis=0)
    key_rows = jnp.concatenate([first_keys[None], before_keys], axis=1)
    value_rows = jnp.concatenate([first_values[None], before_values], axis=1)
    query_rows = space_q.reshape(frames, places, HEADS, HEAD_DIM)
    key_rows = key_rows.reshape(frames, 2 * places, HEADS, HEAD_DIM)
    value_rows = value_rows.reshape(frames, 2 * places, HEADS, HEAD_DIM)
    scores = (
        jnp.einsum("fqhe,fkhe->fhqk", query_rows, key_rows, preferred_element_type=jnp.float32)
        * factor
    )
    weights = softmax_rows(scores)
    space_mix = jnp.einsum(
        "fhqk,fkhe->fqhe", weights, value_rows, preferred_element_type=jnp.float32
    ).astype(jnp.bfloat16)
    space_out = jnp.dot(
        space_mix.reshape(-1, channels), out_space, preferred_element_type=jnp.float32
    ).reshape(frames, places, channels)
    after_space = (latents.astype(jnp.float32) + space_out).astype(jnp.bfloat16)
    normed_two = normalize(after_space)
    onehot = (
        bucket_table[:, None] == jnp.arange(position_bias.shape[1], dtype=jnp.int32)[None, :]
    ).astype(jnp.float32)
    bias_rows = jnp.dot(position_bias, onehot.T, precision=lax.Precision.HIGHEST)
    owners = lax.axis_size("frame")
    share = places // owners
    flat_rows = squeeze_items(
        lax.all_to_all(
            normed_two.reshape(frames, owners, share, channels),
            "frame",
            split_axis=1,
            concat_axis=0,
            tiled=True,
        )
    )
    mixed = temporal_attend(
        project(flat_rows, query_time),
        project(flat_rows, key_time),
        project(flat_rows, value_time),
        bias_rows,
    )
    gathered_mix = mixed[:, None]
    time_mix = lax.all_to_all(
        gathered_mix, "frame", split_axis=0, concat_axis=1, tiled=True
    ).reshape(frames, places, channels)
    time_out = jnp.dot(
        time_mix.reshape(-1, channels), out_time, preferred_element_type=jnp.float32
    ).reshape(frames, places, channels)
    return (after_space.astype(jnp.float32) + time_out).astype(jnp.bfloat16)


def solution(mesh):
    in_specs = (P(("batch", "frame"), None, None), P(), P(), P(), P(), P(), P(), P(), P(), P(), P())
    out_specs = P(("batch", "frame"), None, None)
    return jax.shard_map(body, mesh=mesh, in_specs=in_specs, out_specs=out_specs, check_vma=False)
```

profile of v0, /device:TPU:1, one launch (start us, length us, event | category | flops | bytes accessed | tf_op | source)
XLA Modules:
  0.0 173.2 jit_solution(1357296057770474128)
XLA Ops:
  6.6 1.2 convert_reduce_fusion
  7.8 1.2 fusion.24
  9.0 1.8 %fusion.17 = bf16[1,256,640]{2,1,0:T(8,128)(2,1)S(1)} fusion(bf16[640,640]{1,0:T(8,128)(2,1)} %param.13, bf16[1,256,640]{2,1,0:T(8,128)(2,1)} %param.11, f32[256]{0:T(256)S(1)} %add_rsqrt_fusion.1, f32[256]{0:T(256)S(1)} %broadcast_multiply_fusion.1), kind=kOutput, calls=%fused_computation.29 | convolution fusion | flops 210534400 | bytes 1476608 | tf_op jit(solution)/shard_map/dot_general | solution.py:37
  10.8 1.8 %fusion.18 = bf16[1,256,640]{2,1,0:T(8,128)(2,1)S(1)} fusion(bf16[640,640]{1,0:T(8,128)(2,1)} %param.14, bf16[1,256,640]{2,1,0:T(8,128)(2,1)} %param.11, f32[256]{0:T(256)S(1)} %add_rsqrt_fusion.1, f32[256]{0:T(256)S(1)} %broadcast_multiply_fusion.1), kind=kOutput, calls=%fused_computation.30 | convolution fusion | flops 210534400 | bytes 1476608 | tf_op jit(solution)/shard_map/dot_general | solution.py:37
  12.5 1.0 broadcast_select_fusion
  13.5 4.5 %collective-permute-start = (bf16[2,256,640]{2,1,0:T(8,128)(2,1)S(1)}, bf16[2,256,640]{2,1,0:T(8,128)(2,1)}, u32[]{:S(2)}, u32[]{:S(2)}) collective-permute-start(bf16[2,256,640]{2,1,0:T(8,128)(2,1)S(1)} %get-tuple-element.30), channel_id=1, source_target_pairs={{0,2},{2,4},{4,6},{6,8},{8,10},{10,12},{12,14},{14,16},{16,18},{18... | collective-permute-start | bytes 1966088 | tf_op jit(solution)/shard_map/ppermute | solution.py:18
  18.1 0.5 convolution_convert_fusion.4
  18.8 90.3 %all-reduce.2.cloned.1.call-done = bf16[2,256,640]{2,1,0:T(8,128)(2,1)} async-done(((bf16[2,256,640]{2,1,0:T(8,128)(2,1)}), bf16[2,256,640]{2,1,0:T(8,128)(2,1)}) %all-reduce.2.cloned.1.call-update) | async-done | bytes 655376 | tf_op jit(solution)/shard_map/psum | solution.py:23
  109.1 1.4 slice_select_fusion.1
  110.7 0.2 copy.39
  110.8 0.8 fusion.28
  111.6 1.9 %copy-done.1 = f32[8,256,512]{2,1,0:T(8,128)} copy-done((f32[8,256,512]{2,1,0:T(8,128)}, f32[8,256,512]{2,1,0:T(8,128)S(1)}, u32[]{:S(2)}) %copy-start.1) | copy-done | bytes 4194328
  113.5 1.4 fusion.53
  115.2 7.3 %fusion.16 = bf16[8,80,256]{2,1,0:T(8,128)(2,1)S(1)} fusion(f32[8,256]{1,0:T(8,128)S(1)} %fusion.53, bf16[1,256,8,80]{1,3,2,0:T(8,128)(2,1)S(1)} %bitcast.85, bf16[1,256,8,80]{1,3,2,0:T(8,128)(2,1)S(1)} %bitcast.84, f32[8,256,512]{2,1,0:T(8,128)} %copy-done.1), kind=kOutput, calls=%fused_computation.22 | convolution fusion | flops 174492160 | bytes 5185536 | tf_op jit(solution)/shard_map/fhqk,fkhe->fqhe/dot_general | solution.py:119
  122.6 0.6 fusion.54
  123.1 0.2 multiply_reduce_fusion.1
  123.4 0.9 multiply_convert_fusion
  124.3 5.2 %all-to-all-start = ((bf16[1,16,16,640]{3,2,0,1:T(8,128)(2,1)}), bf16[1,16,16,640]{3,2,0,1:T(8,128)(2,1)S(1)}, u32[]{:S(2)}, u32[]{:S(2)}) async-start(bf16[1,16,16,640]{3,2,0,1:T(8,128)(2,1)} %bitcast.15), calls=%async_computation | async-start | bytes 655360 | tf_op jit(solution)/shard_map/all_to_all | solution.py:134
  129.5 0.2 convolution_bitcast_fusion.2
  129.9 0.7 gather_fusion
  130.8 9.4 %all-to-all-done = bf16[1,16,16,640]{3,2,0,1:T(8,128)(2,1)S(1)} async-done(((bf16[1,16,16,640]{3,2,0,1:T(8,128)(2,1)}), bf16[1,16,16,640]{3,2,0,1:T(8,128)(2,1)S(1)}, u32[]{:S(2)}, u32[]{:S(2)}) %all-to-all-start) | async-done | bytes 327712 | tf_op jit(solution)/shard_map/all_to_all | solution.py:134
  140.2 0.5 convolution_convert_fusion.2
  140.7 0.6 reshape.182
  141.3 1.6 convolution_convert_fusion.1
  142.9 0.6 reshape.183
  143.5 1.6 convolution_convert_fusion.3
  145.1 1.4 reshape.181
  146.5 2.0 %fusion.55 = (f32[16,8,16]{2,1,0:T(8,128)S(1)}, f32[16,8,16,16]{2,3,1,0:T(8,128)}) fusion(bf16[16,16,8,80]{3,2,1,0:T(8,128)(2,1)S(1)} %reshape.183, bf16[16,16,8,80]{3,2,1,0:T(8,128)(2,1)S(1)} %reshape.182, f32[8,16,16]{1,2,0:T(8,128)S(1)} %bitcast.88), kind=kOutput, calls=%fused_computation.78 | convolution fusion | flops 5373967 | bytes 802816 | tf_op jit(solution)/shard_map/while/body/eval_jaxpr/sub | solution.py:43
  148.5 1.9 %fusion.10 = bf16[16,16,8,80]{3,0,2,1:T(8,128)(2,1)S(1)} fusion(f32[16,8,16,16]{2,3,1,0:T(8,128)} %get-tuple-element.35, bf16[16,16,8,80]{3,2,1,0:T(8,128)(2,1)} %reshape.181, f32[16,8,16]{2,1,0:T(8,128)S(1)} %get-tuple-element.34), kind=kOutput, calls=%fused_computation.16 | convolution fusion | flops 5472256 | bytes 794624 | tf_op jit(solution)/shard_map/while/body/eval_jaxpr/phij,jphe->iphe/dot_general | solution.py:68
  150.6 0.4 broadcast_in_dim_reshape.3
  151.0 14.1 %all_to_all.8 = bf16[16,1,16,640]{3,2,1,0:T(8,128)(2,1)S(1)} all-to-all(bf16[16,1,16,640]{3,2,1,0:T(8,128)(2,1)S(1)} %bitcast.82), channel_id=1, replica_groups=mesh['frame'=16,'batch'=2] {'frame'}, dimensions={0} | all-to-all | bytes 655360 | tf_op jit(solution)/shard_map/all_to_all | solution.py:149
  165.1 1.2 fusion.13
  (32 shorter events, 1.3 us)
Async XLA Ops:
  6.5 116.0 %copy-start = (bf16[640,640]{1,0:T(8,128)(2,1)S(1)}, bf16[640,640]{1,0:T(8,128)(2,1)}, u32[]{:S(2)}) copy-start(bf16[640,640]{1,0:T(8,128)(2,1)} %param.15) | copy-start | bytes 2457604
  6.5 11.5 %copy-start.2 = (bf16[1,256,640]{2,1,0:T(8,128)(2,1)S(1)}, bf16[1,256,640]{2,1,0:T(8,128)(2,1)}, u32[]{:S(2)}) copy-start(bf16[1,256,640]{2,1,0:T(8,128)(2,1)} %param.11) | copy-start | bytes 983044
  6.5 11.5 %copy-start.5 = (bf16[640,640]{1,0:T(8,128)(2,1)S(1)}, bf16[640,640]{1,0:T(8,128)(2,1)}, u32[]{:S(2)}) copy-start(bf16[640,640]{1,0:T(8,128)(2,1)} %param.12) | copy-start | bytes 2457604
  6.5 102.6 %all-reduce.2.cloned.1.call-start = ((), (), s32[]{:S(2)}) async-start(), calls=%async_computation.2 | async-start | bytes 1310720 | tf_op jit(solution)/shard_map/psum | solution.py:23
  13.5 95.6 %collective-permute-start = (bf16[2,256,640]{2,1,0:T(8,128)(2,1)S(1)}, bf16[2,256,640]{2,1,0:T(8,128)(2,1)}, u32[]{:S(2)}, u32[]{:S(2)}) collective-permute-start(bf16[2,256,640]{2,1,0:T(8,128)(2,1)S(1)} %get-tuple-element.30), channel_id=1, source_target_pairs={{0,2},{2,4},{4,6},{6,8},{8,10},{10,12},{12,14},{14,16},{16,18},{18... | collective-permute-start | bytes 1966088 | tf_op jit(solution)/shard_map/ppermute | solution.py:18
  111.6 1.9 %copy-start.1 = (f32[8,256,512]{2,1,0:T(8,128)}, f32[8,256,512]{2,1,0:T(8,128)S(1)}, u32[]{:S(2)}) copy-start(f32[8,256,512]{2,1,0:T(8,128)S(1)} %fusion.28) | copy-start | bytes 12582916
  122.5 6.9 %copy-start.6 = (f32[8,32]{1,0:T(8,128)S(1)}, f32[8,32]{1,0:T(8,128)}, u32[]{:S(2)}) copy-start(f32[8,32]{1,0:T(8,128)} %param.20) | copy-start | bytes 3076
  122.5 6.9 %copy-start.7 = (s32[257]{0:T(512)S(1)}, s32[257]{0:T(512)}, u32[]{:S(2)}) copy-start(s32[257]{0:T(512)} %param.21) | copy-start | bytes 3088
  122.5 17.7 %copy-start.3 = (bf16[640,640]{1,0:T(8,128)(2,1)S(1)}, bf16[640,640]{1,0:T(8,128)(2,1)}, u32[]{:S(2)}) copy-start(bf16[640,640]{1,0:T(8,128)(2,1)} %param.16) | copy-start | bytes 2457604
  124.3 16.0 %all-to-all-start = ((bf16[1,16,16,640]{3,2,0,1:T(8,128)(2,1)}), bf16[1,16,16,640]{3,2,0,1:T(8,128)(2,1)S(1)}, u32[]{:S(2)}, u32[]{:S(2)}) async-start(bf16[1,16,16,640]{3,2,0,1:T(8,128)(2,1)} %bitcast.15), calls=%async_computation | async-start | bytes 655360 | tf_op jit(solution)/shard_map/all_to_all | solution.py:134
  148.5 16.6 %copy-start.4 = (bf16[640,640]{1,0:T(8,128)(2,1)S(1)}, bf16[640,640]{1,0:T(8,128)(2,1)}, u32[]{:S(2)}) copy-start(bf16[640,640]{1,0:T(8,128)(2,1)} %param.19) | copy-start | bytes 2457604
Sparse Core Ops, SparseCore 0:
  18.2 90.8 all-reduce.1
where the time goes:
time: 174 us; the launch traced here: 173 us
  waiting for transfers between devices  99.8 us (57%)
  matrix products  21.7 us (12%)
  blocking collectives  14.1 us (8%)
  between operations  13.6 us (8%)
  starting transfers between devices  9.68 us (6%)
  other arithmetic  7.29 us (4%)
  local copies, waits for them, and re-layouts  6.98 us (4%)
    psum x1, waiting for transfers between devices, spread_2(): return lax.psum(block, axis)  90.3 us
    all_to_all x1, blocking collectives, body(): lax.all_to_all(gathered_mix, 'frame', split_axis=0, concat_axis=1, tiled=...  14.1 us
    all_to_all x1, waiting for transfers between devices, body(): lax.all_to_all(normed_two.reshape(frames, owners, share, channels), 'fram...  9.43 us
    dot_general x6, matrix products, project(): result = jnp.dot(flat, weight, preferred_element_type=jnp.float32)  7.7 us
    dot_general x1, matrix products, body(): jnp.einsum('fhqk,fkhe->fqhe', weights, value_rows, preferred_element_type...  7.26 us
    all_to_all x1, starting transfers between devices, body(): lax.all_to_all(normed_two.reshape(frames, owners, share, channels), 'fram...  5.18 us
    ppermute x1, starting transfers between devices, from_behind(): return lax.ppermute(x, axis, pairs)  4.5 us
  transfers between devices with their start and end apart: 3, of which 2 were waited for; matrix products, arithmetic and copies ran while one was open for 1% of the time, Pallas kernels for 0%

commit v1 on v0

--- a/solution.py
+++ b/solution.py
@@ -1,8 +1,11 @@
+import functools
 import math
 
 import jax
 import jax.numpy as jnp
 from jax import lax
+from jax.experimental import pallas as pl
+from jax.experimental.pallas import tpu as pltpu
 from jax.sharding import PartitionSpec as P
 
 HEADS = 8
@@ -155,7 +158,434 @@
     return (after_space.astype(jnp.float32) + time_out).astype(jnp.bfloat16)
 
 
+AXIS = "frame"
+MESH = pl.DeviceIdType.MESH
+LANES = 128
+FAR_BELOW = -1e30
+LOG2E = 1.4426950408889634
+
+
+def windows(channels):
+    spans = []
+    for head in range(HEADS):
+        begin, end = head * HEAD_DIM, (head + 1) * HEAD_DIM
+        low = begin // LANES * LANES
+        high = min(-(-end // LANES) * LANES, channels)
+        spans.append((low, high, begin - low, end - low))
+    return spans
+
+
+def attend(q_ref, k_ref, v_ref, rows, scale, bias_ref):
+    channels = q_ref.shape[-1]
+    tiles = [None] * (channels // LANES)
+    for head, (low, high, begin, end) in enumerate(windows(channels)):
+        lane = lax.broadcasted_iota(jnp.int32, (rows.size, high - low), 1)
+        inside = (lane >= begin) & (lane < end)
+        query = q_ref[rows, low:high]
+        query = jnp.where(inside, query, jnp.zeros_like(query))
+        scores = lax.dot_general(
+            query, k_ref[:, low:high], (((1,), (1,)), ((), ())), preferred_element_type=jnp.float32
+        )
+        if bias_ref is None:
+            highest = jnp.max(scores, axis=-1, keepdims=True)
+            powered = jnp.exp2((scores - highest) * (scale * LOG2E))
+        else:
+            scores = scores * scale + bias_ref[head, rows, :]
+            highest = jnp.max(scores, axis=-1, keepdims=True)
+            powered = jnp.exp2((scores - highest) * LOG2E)
+        total = jnp.sum(powered, axis=-1, keepdims=True)
+        mixed = jnp.dot(
+            powered.astype(jnp.bfloat16), v_ref[:, low:high], preferred_element_type=jnp.float32
+        )
+        mixed = mixed * (1.0 / total)
+        for at in range(low, high, LANES):
+            part = mixed[:, at - low : at - low + LANES]
+            keep = inside[:, at - low : at - low + LANES]
+            old = tiles[at // LANES]
+            tiles[at // LANES] = part if old is None else jnp.where(keep, part, old)
+    return jnp.concatenate([t.astype(jnp.bfloat16) for t in tiles], axis=1)
+
+
+def norm_rows(floats):
+    average = jnp.mean(floats, axis=-1, keepdims=True)
+    centred = floats - average
+    spread = jnp.mean(centred * centred, axis=-1, keepdims=True)
+    return (centred * lax.rsqrt(spread + EPS)).astype(jnp.bfloat16)
+
+
+def matmul(rows, weight):
+    return jnp.dot(rows, weight, preferred_element_type=jnp.float32)
+
+
+def block_kernel(
+    n,
+    share,
+    lat,
+    *refs,
+):
+    weights, refs = refs[:8], refs[8:]
+    pos_bias, buckets, out = refs[:3]
+    (
+        x,
+        w,
+        first,
+        prior,
+        q,
+        k,
+        v,
+        after,
+        go,
+        came,
+        back_go,
+        back_came,
+        bias,
+        x_sem,
+        w_sem,
+        prior_sems,
+        a_send,
+        b_send,
+        c_send,
+        first_recv,
+        go_send,
+        go_recv,
+        back_send,
+        back_recv,
+    ) = refs[3:]
+    me = lax.axis_index(AXIS)
+    places, channels = x.shape
+    scale = 1.0 / math.sqrt(HEAD_DIM)
+    other = lax.rem(me + 1, n)
+
+    barrier = pltpu.get_barrier_semaphore()
+
+    @pl.loop(1, n)
+    def _(step):
+        pl.semaphore_signal(
+            barrier, inc=1, device_id={AXIS: lax.rem(me + step, n)}, device_id_type=MESH
+        )
+
+    own = pltpu.make_async_copy(lat.at[0], x, x_sem)
+    own.start()
+    loads = [pltpu.make_async_copy(weights[i], w.at[i], w_sem.at[i]) for i in range(8)]
+    for load in loads:
+        load.start()
+
+    onehot = (
+        lax.broadcasted_iota(jnp.int32, (pos_bias.shape[1], 256), 0) == buckets[:, 0:256]
+    ).astype(jnp.float32)
+    by_offset = jnp.dot(
+        pos_bias[...], onehot, precision=lax.Precision.HIGHEST, preferred_element_type=jnp.float32
+    )
+    limit = (buckets.shape[1] - 1) // 2
+    wide = 2 * n * share
+    pick = (
+        lax.broadcasted_iota(jnp.int32, (256, wide), 0)
+        == lax.broadcasted_iota(jnp.int32, (256, wide), 1) // share + (limit - (n - 1))
+    ).astype(jnp.float32)
+    spread = jnp.dot(
+        by_offset, pick, precision=lax.Precision.HIGHEST, preferred_element_type=jnp.float32
+    )
+    same = lax.broadcasted_iota(jnp.int32, (share, n * share), 0) == lax.rem(
+        lax.broadcasted_iota(jnp.int32, (share, n * share), 1), share
+    )
+    for i in range(n):
+        begin = (n - 1 - i) * share
+        line = spread[:, begin : begin + n * share]
+        for head in range(HEADS):
+            bias[head, i * share : (i + 1) * share, :] = jnp.where(
+                same, line[head : head + 1, :], FAR_BELOW
+            )
+
+    pl.semaphore_wait(barrier, n - 1)
+
+    def chunk(c):
+        return lat.at[0, pl.ds(pl.multiple_of(c * share, share), share), :]
+
+    def scatter(c):
+        return pltpu.make_async_remote_copy(
+            chunk(c), first.at[c], a_send.at[c], first_recv.at[c], {AXIS: c}, MESH
+        )
+
+    def gather(c, to):
+        return pltpu.make_async_remote_copy(
+            first.at[c], first.at[c], b_send.at[to], first_recv.at[c], {AXIS: to}, MESH
+        )
+
+    sibling = me + 1 - 2 * lax.rem(me, 2)
+
+    def pair(c):
+        return pltpu.make_async_remote_copy(
+            first.at[c], first.at[c], c_send.at[c], first_recv.at[c], {AXIS: sibling}, MESH
+        )
+
+    send_prior = pltpu.make_async_remote_copy(
+        lat.at[0], prior, prior_sems.at[0], prior_sems.at[1], {AXIS: other}, MESH
+    )
+
+    @pl.when(me == 0)
+    def _():
+        @pl.loop(1, n)
+        def _(step):
+            scatter(n - step).start()
+
+    @pl.when(me < n - 1)
+    def _():
+        send_prior.start()
+
+    own.wait()
+
+    @pl.when(me == 0)
+    def _():
+        prior[...] = x[...]
+        first[...] = x[...].reshape(n, share, channels)
+
+    def took(c):
+        pltpu.make_async_remote_copy(
+            first.at[c], first.at[c], b_send.at[0], first_recv.at[c], {AXIS: other}, MESH
+        ).wait_recv()
+
+    @pl.when(me > 0)
+    def _():
+        took(me)
+
+    @pl.loop(1, n // 2)
+    def _(step):
+        to = lax.rem(me + 2 * step, n)
+
+        @pl.when(to != 0)
+        def _():
+            gather(me, to).start()
+
+    @pl.when(sibling != 0)
+    def _():
+        pair(me).start()
+
+    normed = norm_rows(x[...].astype(jnp.float32))
+    loads[0].wait()
+    q[...] = matmul(normed, w[0]).astype(jnp.bfloat16)
+
+    @pl.loop(1, n // 2)
+    def _(step):
+        c = lax.rem(me + n - 2 * step, n)
+
+        @pl.when(me > 0)
+        def _():
+            took(c)
+
+        @pl.when(sibling != 0)
+        def _():
+            pair(c).start()
+
+    @pl.when(me > 0)
+    def _():
+        pltpu.make_async_remote_copy(
+            lat.at[0], prior, prior_sems.at[0], prior_sems.at[1], {AXIS: other}, MESH
+        ).wait_recv()
+
+    normed = norm_rows(prior[...].astype(jnp.float32))
+    loads[1].wait()
+    loads[2].wait()
+    k[places:, :] = matmul(normed, w[1]).astype(jnp.bfloat16)
+    v[places:, :] = matmul(normed, w[2]).astype(jnp.bfloat16)
+
+    @pl.when(me > 0)
+    def _():
+        @pl.loop(0, n // 2)
+        def _(step):
+            took(2 * step + lax.rem(me + 1, 2))
+
+    normed = norm_rows(first[...].reshape(places, channels).astype(jnp.float32))
+    k[:places, :] = matmul(normed, w[1]).astype(jnp.bfloat16)
+    v[:places, :] = matmul(normed, w[2]).astype(jnp.bfloat16)
+
+    for i in range(3, 8):
+        loads[i].wait()
+
+    halves = 2
+    size = places // halves
+
+    def to_owner(to):
+        return pltpu.make_async_remote_copy(
+            go.at[to], came.at[me], go_send.at[to], go_recv.at[me], {AXIS: to}, MESH
+        )
+
+    def to_frame(to):
+        return pltpu.make_async_remote_copy(
+            back_go.at[to], back_came.at[me], back_send.at[to], back_recv.at[me], {AXIS: to}, MESH
+        )
+
+    def start_group(make, half):
+        count = n // halves
+
+        @pl.loop(0, count)
+        def _(step):
+            to = half * count + lax.rem(me + step, count)
+
+            @pl.when(to != me)
+            def _():
+                make(to).start()
+
+    def space_block(half):
+        rows = pl.ds(pl.multiple_of(half * size, size), size)
+        mix = attend(q, k, v, rows, scale, None)
+        summed = x[rows, :].astype(jnp.float32) + matmul(mix, w[3])
+        rounded = summed.astype(jnp.bfloat16)
+        after[rows, :] = rounded
+        go[pl.ds(half * (n // halves), n // halves)] = norm_rows(
+            rounded.astype(jnp.float32)
+        ).reshape(n // halves, share, channels)
+        start_group(to_owner, half)
+
+    pl.loop(0, halves)(space_block)
+
+    came[pl.ds(me, 1)] = go[pl.ds(me, 1)]
+
+    @pl.loop(1, n)
+    def _(step):
+        c = lax.rem(me + step, n)
+        pltpu.make_async_remote_copy(
+            came.at[c], came.at[c], go_send.at[c], go_recv.at[c], {AXIS: c}, MESH
+        ).wait_recv()
+
+    rows = came[...].reshape(n * share, channels)
+    q[...] = matmul(rows, w[4]).astype(jnp.bfloat16)
+    k[:places, :] = matmul(rows, w[5]).astype(jnp.bfloat16)
+    v[:places, :] = matmul(rows, w[6]).astype(jnp.bfloat16)
+
+    def time_block(half):
+        rows = pl.ds(pl.multiple_of(half * size, size), size)
+        mix = attend(q, k.at[:places], v.at[:places], rows, scale, bias)
+        back_go[pl.ds(half * (n // halves), n // halves)] = mix.reshape(
+            n // halves, share, channels
+        )
+        start_group(to_frame, half)
+
+    pl.loop(0, halves)(time_block)
+
+    back_came[pl.ds(me, 1)] = back_go[pl.ds(me, 1)]
+
+    @pl.loop(1, n)
+    def _(step):
+        c = lax.rem(me + step, n)
+        pltpu.make_async_remote_copy(
+            back_came.at[c], back_came.at[c], back_send.at[c], back_recv.at[c], {AXIS: c}, MESH
+        ).wait_recv()
+
+    mix = back_came[...].reshape(places, channels)
+    out[0] = (after[...].astype(jnp.float32) + matmul(mix, w[7])).astype(jnp.bfloat16)
+
+    @pl.when(me == 0)
+    def _():
+        @pl.loop(1, n)
+        def _(step):
+            scatter(n - step).wait_send()
+
+    @pl.when(me < n - 1)
+    def _():
+        send_prior.wait_send()
+
+    @pl.loop(1, n // 2)
+    def _(step):
+        to = lax.rem(me + 2 * step, n)
+
+        @pl.when(to != 0)
+        def _():
+            gather(me, to).wait_send()
+
+    @pl.when(sibling != 0)
+    def _():
+        @pl.loop(0, n // 2)
+        def _(step):
+            pair(lax.rem(me + 2 * step, n)).wait_send()
+
+    @pl.loop(1, n)
+    def _(step):
+        c = lax.rem(me + step, n)
+        to_owner(c).wait_send()
+        to_frame(c).wait_send()
+
+
+def kernel_body(
+    latents,
+    query_space,
+    key_space,
+    value_space,
+    out_space,
+    query_time,
+    key_time,
+    value_time,
+    out_time,
+    position_bias,
+    bucket_table,
+):
+    _, places, channels = latents.shape
+    n = lax.axis_size(AXIS)
+    share = places // n
+    rows = n * share
+    bf16 = jnp.bfloat16
+    anywhere = pl.BlockSpec(memory_space=pl.ANY)
+    vmem = pl.BlockSpec(memory_space=pltpu.VMEM)
+    blocks = pltpu.VMEM((n, share, channels), bf16)
+    plane = pltpu.VMEM((places, channels), bf16)
+    dma = pltpu.SemaphoreType.DMA
+    return pl.pallas_call(
+        functools.partial(block_kernel, n, share),
+        out_shape=jax.ShapeDtypeStruct(latents.shape, bf16),
+        in_specs=[anywhere] * 9 + [vmem] * 2,
+        out_specs=vmem,
+        scratch_shapes=[
+            plane,
+            pltpu.VMEM((8, channels, channels), bf16),
+            blocks,
+            plane,
+            plane,
+            pltpu.VMEM((2 * places, channels), bf16),
+            pltpu.VMEM((2 * places, channels), bf16),
+            plane,
+            blocks,
+            blocks,
+            blocks,
+            blocks,
+            pltpu.VMEM((HEADS, rows, rows), jnp.float32),
+            dma,
+            dma((8,)),
+            dma((2,)),
+            dma((n,)),
+            dma((n,)),
+            dma((n,)),
+            dma((n,)),
+            dma((n,)),
+            dma((n,)),
+            dma((n,)),
+            dma((n,)),
+        ],
+        compiler_params=pltpu.CompilerParams(
+            collective_id=0, has_side_effects=True, vmem_limit_bytes=48 * 1024 * 1024
+        ),
+    )(
+        latents,
+        query_space,
+        key_space,
+        value_space,
+        out_space,
+        query_time,
+        key_time,
+        value_time,
+        out_time,
+        position_bias,
+        bucket_table.reshape(1, -1),
+    )
+
+
+def one_kernel(latents, *rest):
+    frames, places, _ = latents.shape
+    n = lax.axis_size(AXIS)
+    limit = (rest[-1].shape[0] - 1) // 2
+    fits = frames == 1 and n % 2 == 0 and places % (16 * n) == 0 and limit + n <= 256 and n <= limit
+    return (kernel_body if fits else body)(latents, *rest)
+
+
 def solution(mesh):
     in_specs = (P(("batch", "frame"), None, None), P(), P(), P(), P(), P(), P(), P(), P(), P(), P())
     out_specs = P(("batch", "frame"), None, None)
-    return jax.shard_map(body, mesh=mesh, in_specs=in_specs, out_specs=out_specs, check_vma=False)
+    return jax.shard_map(one_kernel, mesh=mesh, in_specs=in_specs, out_specs=out_specs, check_vma=False)

time: 174 us -> 55.5 us (0.32)
  waiting for transfers between devices: 99.8 us -> 0 us
  Pallas kernels: 0 us -> 44.6 us
  matrix products: 21.7 us -> 0 us
  blocking collectives: 14.1 us -> 0 us
  between operations: 13.6 us -> 0.02 us
  starting transfers between devices: 9.68 us -> 0 us
  other arithmetic: 7.29 us -> 0 us
  local copies, waits for them, and re-layouts: 6.98 us -> 9.93 us
    psum x1 -> x0, waiting for transfers between devices: 90.3 us -> none  [spread_2(): return lax.psum(block, axis)]
    pallas_call x0 -> x1, Pallas kernels: none -> 44.6 us  [kernel_body(): pl.pallas_call(functools.partial(block_kernel, n, share), out_shape=jax.S...]
    dot_general x12 -> x0, matrix products: 19.7 us -> none  [the longest x6 7.7 us: project(): result = jnp.dot(flat, weight, preferred_element_type=jnp.float32)]
    all_to_all x1 -> x0, blocking collectives: 14.1 us -> none  [body(): lax.all_to_all(gathered_mix, 'frame', split_axis=0, concat_axis=1, tiled=...]
    all_to_all x1 -> x0, waiting for transfers between devices: 9.43 us -> none  [body(): lax.all_to_all(normed_two.reshape(frames, owners, share, channels), 'fram...]
    unnamed x16 -> x17, local copies, waits for them, and re-layouts: 1.95 us -> 9.25 us
    all_to_all x1 -> x0, starting transfers between devices: 5.18 us -> none  [body(): lax.all_to_all(normed_two.reshape(frames, owners, share, channels), 'fram...]
    ppermute x1 -> x0, starting transfers between devices: 4.5 us -> none  [from_behind(): return lax.ppermute(x, axis, pairs)]
  transfers between devices with their start and end apart: 3 -> 0, of which waited for: 2 -> 0; matrix products, arithmetic and copies ran while one was open for 1% -> 0% of each run, Pallas kernels for 0% -> 0%
where the time goes in v1:
time: 55.5 us; the launch traced here: 54.6 us
  Pallas kernels  44.6 us (80%)
  local copies, waits for them, and re-layouts  9.93 us (18%)
    pallas_call x1, Pallas kernels, kernel_body(): pl.pallas_call(functools.partial(block_kernel, n, share), out_shape=jax.S...  44.6 us
    unnamed x17, local copies, waits for them, and re-layouts  9.25 us

profile of v1, /device:TPU:1, one launch (start us, length us, event | category | flops | bytes accessed | tf_op | source)
XLA Modules:
  0.0 54.6 jit_solution(12325286936204232410)
XLA Ops:
  0.0 0.7 %reshape.3.refs_9_ = s32[1,257]{1,0:T(1,128)S(1)} reshape(s32[257]{0:T(512)} %param.21) | data formatting | bytes 2056 | tf_op jit(solution)/shard_map/reshape | solution.py:576
  0.7 0.0 copy-start
  0.7 1.1 %copy-done = bf16[640,640]{1,0:T(8,128)(2,1)S(1)} copy-done((bf16[640,640]{1,0:T(8,128)(2,1)S(1)}, bf16[640,640]{1,0:T(8,128)(2,1)}, u32[]{:S(2)}) %copy-start) | copy-done | bytes 819224
  1.8 0.0 copy-start.1
  1.8 1.1 %copy-done.1 = bf16[640,640]{1,0:T(8,128)(2,1)S(1)} copy-done((bf16[640,640]{1,0:T(8,128)(2,1)S(1)}, bf16[640,640]{1,0:T(8,128)(2,1)}, u32[]{:S(2)}) %copy-start.1) | copy-done | bytes 819224
  3.0 0.0 copy-start.2
  3.0 1.1 %copy-done.2 = bf16[640,640]{1,0:T(8,128)(2,1)S(1)} copy-done((bf16[640,640]{1,0:T(8,128)(2,1)S(1)}, bf16[640,640]{1,0:T(8,128)(2,1)}, u32[]{:S(2)}) %copy-start.2) | copy-done | bytes 819224
  4.1 0.0 copy-start.3
  4.1 1.1 %copy-done.3 = bf16[640,640]{1,0:T(8,128)(2,1)S(1)} copy-done((bf16[640,640]{1,0:T(8,128)(2,1)S(1)}, bf16[640,640]{1,0:T(8,128)(2,1)}, u32[]{:S(2)}) %copy-start.3) | copy-done | bytes 819224
  5.3 0.0 copy-start.4
  5.3 1.1 %copy-done.4 = bf16[640,640]{1,0:T(8,128)(2,1)S(1)} copy-done((bf16[640,640]{1,0:T(8,128)(2,1)S(1)}, bf16[640,640]{1,0:T(8,128)(2,1)}, u32[]{:S(2)}) %copy-start.4) | copy-done | bytes 819224
  6.4 0.0 copy-start.5
  6.4 1.1 %copy-done.5 = bf16[640,640]{1,0:T(8,128)(2,1)S(1)} copy-done((bf16[640,640]{1,0:T(8,128)(2,1)S(1)}, bf16[640,640]{1,0:T(8,128)(2,1)}, u32[]{:S(2)}) %copy-start.5) | copy-done | bytes 819224
  7.6 0.0 copy-start.6
  7.6 1.0 %copy-done.6 = bf16[1,256,640]{2,1,0:T(8,128)(2,1)S(1)} copy-done((bf16[1,256,640]{2,1,0:T(8,128)(2,1)S(1)}, bf16[1,256,640]{2,1,0:T(8,128)(2,1)}, u32[]{:S(2)}) %copy-start.6) | copy-done | bytes 327704
  8.5 0.0 copy-start.7
  8.5 0.7 %copy-done.7 = f32[8,32]{1,0:T(8,128)S(1)} copy-done((f32[8,32]{1,0:T(8,128)S(1)}, f32[8,32]{1,0:T(8,128)}, u32[]{:S(2)}) %copy-start.7) | copy-done | bytes 1048
  9.2 44.6 %shard_map.109 = bf16[1,256,640]{2,1,0:T(8,128)(2,1)S(1)} custom-call(bf16[1,256,640]{2,1,0:T(8,128)(2,1)S(1)} %copy-done.6, bf16[640,640]{1,0:T(8,128)(2,1)S(1)} %copy-done, bf16[640,640]{1,0:T(8,128)(2,1)S(1)} %copy-done.1, bf16[640,640]{1,0:T(8,128)(2,1)S(1)} %copy-done.2, bf16[640,640]{1,0:T(8,128)(2,1)S(1)} %copy-done.3, ...), custom_call_target="tpu_custom_call" | custom-call | tf_op jit(solution)/shard_map/pallas_call | solution.py:531
  53.9 0.7 %copy.13 = bf16[1,256,640]{2,1,0:T(8,128)(2,1)} copy(bf16[1,256,640]{2,1,0:T(8,128)(2,1)S(1)} %shard_map.109) | data formatting | bytes 655360
Async XLA Ops:
  0.7 1.1 %copy-start = (bf16[640,640]{1,0:T(8,128)(2,1)S(1)}, bf16[640,640]{1,0:T(8,128)(2,1)}, u32[]{:S(2)}) copy-start(bf16[640,640]{1,0:T(8,128)(2,1)} %refs_0_.1) | copy-start | bytes 2457604
  1.8 1.1 %copy-start.1 = (bf16[640,640]{1,0:T(8,128)(2,1)S(1)}, bf16[640,640]{1,0:T(8,128)(2,1)}, u32[]{:S(2)}) copy-start(bf16[640,640]{1,0:T(8,128)(2,1)} %refs_1_.1) | copy-start | bytes 2457604
  3.0 1.1 %copy-start.2 = (bf16[640,640]{1,0:T(8,128)(2,1)S(1)}, bf16[640,640]{1,0:T(8,128)(2,1)}, u32[]{:S(2)}) copy-start(bf16[640,640]{1,0:T(8,128)(2,1)} %refs_2_.1) | copy-start | bytes 2457604
  4.1 1.1 %copy-start.3 = (bf16[640,640]{1,0:T(8,128)(2,1)S(1)}, bf16[640,640]{1,0:T(8,128)(2,1)}, u32[]{:S(2)}) copy-start(bf16[640,640]{1,0:T(8,128)(2,1)} %refs_3_.1) | copy-start | bytes 2457604
  5.3 1.1 %copy-start.4 = (bf16[640,640]{1,0:T(8,128)(2,1)S(1)}, bf16[640,640]{1,0:T(8,128)(2,1)}, u32[]{:S(2)}) copy-start(bf16[640,640]{1,0:T(8,128)(2,1)} %refs_4_.1) | copy-start | bytes 2457604
  6.4 1.1 %copy-start.5 = (bf16[640,640]{1,0:T(8,128)(2,1)S(1)}, bf16[640,640]{1,0:T(8,128)(2,1)}, u32[]{:S(2)}) copy-start(bf16[640,640]{1,0:T(8,128)(2,1)} %refs_5_.1) | copy-start | bytes 2457604
  7.6 1.0 %copy-start.6 = (bf16[1,256,640]{2,1,0:T(8,128)(2,1)S(1)}, bf16[1,256,640]{2,1,0:T(8,128)(2,1)}, u32[]{:S(2)}) copy-start(bf16[1,256,640]{2,1,0:T(8,128)(2,1)} %lat.1) | copy-start | bytes 983044
  8.5 0.7 %copy-start.7 = (f32[8,32]{1,0:T(8,128)S(1)}, f32[8,32]{1,0:T(8,128)}, u32[]{:S(2)}) copy-start(f32[8,32]{1,0:T(8,128)} %refs_8_.1) | copy-start | bytes 3076

commit v2 on v1

--- a/solution.py
+++ b/solution.py
@@ -224,7 +224,7 @@
     *refs,
 ):
     weights, refs = refs[:8], refs[8:]
-    pos_bias, buckets, out = refs[:3]
+    bias_table, bucket_row, out = refs[:3]
     (
         x,
         w,
@@ -239,8 +239,11 @@
         back_go,
         back_came,
         bias,
+        pos_bias,
+        buckets,
         x_sem,
         w_sem,
+        t_sem,
         prior_sems,
         a_send,
         b_send,
@@ -266,35 +269,15 @@
 
     own = pltpu.make_async_copy(lat.at[0], x, x_sem)
     own.start()
+    tables = [
+        pltpu.make_async_copy(bias_table, pos_bias, t_sem.at[0]),
+        pltpu.make_async_copy(bucket_row, buckets, t_sem.at[1]),
+    ]
+    for table in tables:
+        table.start()
     loads = [pltpu.make_async_copy(weights[i], w.at[i], w_sem.at[i]) for i in range(8)]
     for load in loads:
         load.start()
-
-    onehot = (
-        lax.broadcasted_iota(jnp.int32, (pos_bias.shape[1], 256), 0) == buckets[:, 0:256]
-    ).astype(jnp.float32)
-    by_offset = jnp.dot(
-        pos_bias[...], onehot, precision=lax.Precision.HIGHEST, preferred_element_type=jnp.float32
-    )
-    limit = (buckets.shape[1] - 1) // 2
-    wide = 2 * n * share
-    pick = (
-        lax.broadcasted_iota(jnp.int32, (256, wide), 0)
-        == lax.broadcasted_iota(jnp.int32, (256, wide), 1) // share + (limit - (n - 1))
-    ).astype(jnp.float32)
-    spread = jnp.dot(
-        by_offset, pick, precision=lax.Precision.HIGHEST, preferred_element_type=jnp.float32
-    )
-    same = lax.broadcasted_iota(jnp.int32, (share, n * share), 0) == lax.rem(
-        lax.broadcasted_iota(jnp.int32, (share, n * share), 1), share
-    )
-    for i in range(n):
-        begin = (n - 1 - i) * share
-        line = spread[:, begin : begin + n * share]
-        for head in range(HEADS):
-            bias[head, i * share : (i + 1) * share, :] = jnp.where(
-                same, line[head : head + 1, :], FAR_BELOW
-            )
 
     pl.semaphore_wait(barrier, n - 1)
 
@@ -439,6 +422,35 @@
     pl.loop(0, halves)(space_block)
 
     came[pl.ds(me, 1)] = go[pl.ds(me, 1)]
+
+    for table in tables:
+        table.wait()
+
+    onehot = (
+        lax.broadcasted_iota(jnp.int32, (pos_bias.shape[1], 256), 0) == buckets[0:256].reshape(1, 256)
+    ).astype(jnp.float32)
+    by_offset = jnp.dot(
+        pos_bias[...], onehot, precision=lax.Precision.HIGHEST, preferred_element_type=jnp.float32
+    )
+    limit = (buckets.shape[0] - 1) // 2
+    wide = 2 * n * share
+    pick = (
+        lax.broadcasted_iota(jnp.int32, (256, wide), 0)
+        == lax.broadcasted_iota(jnp.int32, (256, wide), 1) // share + (limit - (n - 1))
+    ).astype(jnp.float32)
+    spread = jnp.dot(
+        by_offset, pick, precision=lax.Precision.HIGHEST, preferred_element_type=jnp.float32
+    )
+    same = lax.broadcasted_iota(jnp.int32, (share, n * share), 0) == lax.rem(
+        lax.broadcasted_iota(jnp.int32, (share, n * share), 1), share
+    )
+    for i in range(n):
+        begin = (n - 1 - i) * share
+        line = spread[:, begin : begin + n * share]
+        for head in range(HEADS):
+            bias[head, i * share : (i + 1) * share, :] = jnp.where(
+                same, line[head : head + 1, :], FAR_BELOW
+            )
 
     @pl.loop(1, n)
     def _(step):
@@ -523,7 +535,7 @@
     share = places // n
     rows = n * share
     bf16 = jnp.bfloat16
-    anywhere = pl.BlockSpec(memory_space=pl.ANY)
+    anywhere = pl.BlockSpec(memory_space=pltpu.HBM)
     vmem = pl.BlockSpec(memory_space=pltpu.VMEM)
     blocks = pltpu.VMEM((n, share, channels), bf16)
     plane = pltpu.VMEM((places, channels), bf16)
@@ -531,7 +543,7 @@
     return pl.pallas_call(
         functools.partial(block_kernel, n, share),
         out_shape=jax.ShapeDtypeStruct(latents.shape, bf16),
-        in_specs=[anywhere] * 9 + [vmem] * 2,
+        in_specs=[anywhere] * 11,
         out_specs=vmem,
         scratch_shapes=[
             plane,
@@ -547,9 +559,12 @@
             blocks,
             blocks,
             pltpu.VMEM((HEADS, rows, rows), jnp.float32),
+            pltpu.VMEM(position_bias.shape, jnp.float32),
+            pltpu.VMEM(bucket_table.shape, jnp.int32),
             dma,
             dma((8,)),
             dma((2,)),
+            dma((2,)),
             dma((n,)),
             dma((n,)),
             dma((n,)),
@@ -560,7 +575,7 @@
             dma((n,)),
         ],
         compiler_params=pltpu.CompilerParams(
-            collective_id=0, has_side_effects=True, vmem_limit_bytes=48 * 1024 * 1024
+            collective_id=0, has_side_effects=True, vmem_limit_bytes=63 * 1024 * 1024
         ),
     )(
         latents,
@@ -573,7 +588,7 @@
         value_time,
         out_time,
         position_bias,
-        bucket_table.reshape(1, -1),
+        bucket_table,
     )
 
 

time: 55.5 us -> 47.9 us (0.86)
  local copies, waits for them, and re-layouts: 9.93 us -> 1.73 us
  Pallas kernels: 44.6 us -> 45.6 us
    unnamed x17 -> x1, local copies, waits for them, and re-layouts: 9.25 us -> 1.73 us
    pallas_call x1, Pallas kernels: 44.6 us -> 45.6 us  [kernel_body(): pl.pallas_call(functools.partial(block_kernel, n, share), out_shape=jax.S...]
    reshape x1 -> x0, local copies, waits for them, and re-layouts: 0.68 us -> none  [kernel_body(): bucket_table.reshape(1, -1)]
where the time goes in v2:
time: 47.9 us; the launch traced here: 47.4 us
  Pallas kernels  45.6 us (95%)
  local copies, waits for them, and re-layouts  1.73 us (4%)
    pallas_call x1, Pallas kernels, kernel_body(): pl.pallas_call(functools.partial(block_kernel, n, share), out_shape=jax.S...  45.6 us
    unnamed x1, local copies, waits for them, and re-layouts  1.73 us

profile of v2, /device:TPU:1, one launch (start us, length us, event | category | flops | bytes accessed | tf_op | source)
XLA Modules:
  0.0 47.4 jit_solution(3668676925094333760)
XLA Ops:
  0.0 45.6 %shard_map.109 = bf16[1,256,640]{2,1,0:T(8,128)(2,1)} custom-call(bf16[1,256,640]{2,1,0:T(8,128)(2,1)} %lat.1, bf16[640,640]{1,0:T(8,128)(2,1)} %refs_0_.1, bf16[640,640]{1,0:T(8,128)(2,1)} %refs_1_.1, bf16[640,640]{1,0:T(8,128)(2,1)} %refs_2_.1, bf16[640,640]{1,0:T(8,128)(2,1)} %refs_3_.1, bf16[640,640]{1,0:T(8,128)(2,1)} %refs_4_.1, ...), custom_call_target="tpu_custom_call" | custom-call | tf_op jit(solution)/shard_map/pallas_call | solution.py:543
  45.6 1.7 %copy.13 = bf16[1,256,640]{2,1,0:T(8,128)(2,1)} copy(bf16[1,256,640]{2,1,0:T(8,128)(2,1)} %shard_map.109) | data formatting | bytes 655360

commit v3 on v2

--- a/solution.py
+++ b/solution.py
@@ -387,14 +387,22 @@
     halves = 2
     size = places // halves
 
+    def place(device):
+        return lax.rem(device, 2) * (n // 2) + device // 2
+
     def to_owner(to):
         return pltpu.make_async_remote_copy(
-            go.at[to], came.at[me], go_send.at[to], go_recv.at[me], {AXIS: to}, MESH
+            go.at[place(to)], came.at[me], go_send.at[to], go_recv.at[me], {AXIS: to}, MESH
         )
 
     def to_frame(to):
         return pltpu.make_async_remote_copy(
-            back_go.at[to], back_came.at[me], back_send.at[to], back_recv.at[me], {AXIS: to}, MESH
+            back_go.at[place(to)],
+            back_came.at[place(me)],
+            back_send.at[to],
+            back_recv.at[me],
+            {AXIS: to},
+            MESH,
         )
 
     def start_group(make, half):
@@ -402,7 +410,7 @@
 
         @pl.loop(0, count)
         def _(step):
-            to = half * count + lax.rem(me + step, count)
+            to = 2 * lax.rem(me // 2 + step, count) + half
 
             @pl.when(to != me)
             def _():
@@ -421,7 +429,7 @@
 
     pl.loop(0, halves)(space_block)
 
-    came[pl.ds(me, 1)] = go[pl.ds(me, 1)]
+    came[pl.ds(me, 1)] = go[pl.ds(place(me), 1)]
 
     for table in tables:
         table.wait()
@@ -444,11 +452,12 @@
     same = lax.broadcasted_iota(jnp.int32, (share, n * share), 0) == lax.rem(
         lax.broadcasted_iota(jnp.int32, (share, n * share), 1), share
     )
-    for i in range(n):
+    order = list(range(0, n, 2)) + list(range(1, n, 2))
+    for block, i in enumerate(order):
         begin = (n - 1 - i) * share
         line = spread[:, begin : begin + n * share]
         for head in range(HEADS):
-            bias[head, i * share : (i + 1) * share, :] = jnp.where(
+            bias[head, block * share : (block + 1) * share, :] = jnp.where(
                 same, line[head : head + 1, :], FAR_BELOW
             )
 
@@ -460,7 +469,8 @@
         ).wait_recv()
 
     rows = came[...].reshape(n * share, channels)
-    q[...] = matmul(rows, w[4]).astype(jnp.bfloat16)
+    ordered = jnp.concatenate([came[i] for i in order], axis=0)
+    q[...] = matmul(ordered, w[4]).astype(jnp.bfloat16)
     k[:places, :] = matmul(rows, w[5]).astype(jnp.bfloat16)
     v[:places, :] = matmul(rows, w[6]).astype(jnp.bfloat16)
 
@@ -474,13 +484,18 @@
 
     pl.loop(0, halves)(time_block)
 
-    back_came[pl.ds(me, 1)] = back_go[pl.ds(me, 1)]
+    back_came[pl.ds(place(me), 1)] = back_go[pl.ds(place(me), 1)]
 
     @pl.loop(1, n)
     def _(step):
         c = lax.rem(me + step, n)
         pltpu.make_async_remote_copy(
-            back_came.at[c], back_came.at[c], back_send.at[c], back_recv.at[c], {AXIS: c}, MESH
+            back_came.at[place(c)],
+            back_came.at[place(c)],
+            back_send.at[c],
+            back_recv.at[c],
+            {AXIS: c},
+            MESH,
         ).wait_recv()
 
     mix = back_came[...].reshape(places, channels)

time: 47.9 us -> 44 us (0.919)
  Pallas kernels: 45.6 us -> 42.2 us
    pallas_call x1, Pallas kernels: 45.6 us -> 42.2 us  [kernel_body(): pl.pallas_call(functools.partial(block_kernel, n, share), out_shape=jax.S...]
where the time goes in v3:
time: 44 us; the launch traced here: 43.9 us
  Pallas kernels  42.2 us (96%)
  local copies, waits for them, and re-layouts  1.73 us (4%)
    pallas_call x1, Pallas kernels, kernel_body(): pl.pallas_call(functools.partial(block_kernel, n, share), out_shape=jax.S...  42.2 us
    unnamed x1, local copies, waits for them, and re-layouts  1.73 us

profile of v3, /device:TPU:1, one launch (start us, length us, event | category | flops | bytes accessed | tf_op | source)
XLA Modules:
  0.0 43.9 jit_solution(4891403736753592146)
XLA Ops:
  0.0 42.2 %shard_map.109 = bf16[1,256,640]{2,1,0:T(8,128)(2,1)} custom-call(bf16[1,256,640]{2,1,0:T(8,128)(2,1)} %lat.1, bf16[640,640]{1,0:T(8,128)(2,1)} %refs_0_.1, bf16[640,640]{1,0:T(8,128)(2,1)} %refs_1_.1, bf16[640,640]{1,0:T(8,128)(2,1)} %refs_2_.1, bf16[640,640]{1,0:T(8,128)(2,1)} %refs_3_.1, bf16[640,640]{1,0:T(8,128)(2,1)} %refs_4_.1, ...), custom_call_target="tpu_custom_call" | custom-call | tf_op jit(solution)/shard_map/pallas_call | solution.py:558
  42.2 1.7 %copy.13 = bf16[1,256,640]{2,1,0:T(8,128)(2,1)} copy(bf16[1,256,640]{2,1,0:T(8,128)(2,1)} %shard_map.109) | data formatting | bytes 655360

commit v4 on v3

--- a/solution.py
+++ b/solution.py
@@ -384,11 +384,11 @@
     for i in range(3, 8):
         loads[i].wait()
 
-    halves = 2
+    halves = 4
     size = places // halves
 
     def place(device):
-        return lax.rem(device, 2) * (n // 2) + device // 2
+        return lax.rem(device + device // 4, 4) * (n // 4) + device // 4
 
     def to_owner(to):
         return pltpu.make_async_remote_copy(
@@ -410,7 +410,8 @@
 
         @pl.loop(0, count)
         def _(step):
-            to = 2 * lax.rem(me // 2 + step, count) + half
+            far = lax.rem(me // 4 + step, count)
+            to = 4 * far + lax.rem(half + 3 * far, 4)
 
             @pl.when(to != me)
             def _():
@@ -452,7 +453,7 @@
     same = lax.broadcasted_iota(jnp.int32, (share, n * share), 0) == lax.rem(
         lax.broadcasted_iota(jnp.int32, (share, n * share), 1), share
     )
-    order = list(range(0, n, 2)) + list(range(1, n, 2))
+    order = [4 * far + (group - far) % 4 for group in range(4) for far in range(n // 4)]
     for block, i in enumerate(order):
         begin = (n - 1 - i) * share
         line = spread[:, begin : begin + n * share]
@@ -611,7 +612,7 @@
     frames, places, _ = latents.shape
     n = lax.axis_size(AXIS)
     limit = (rest[-1].shape[0] - 1) // 2
-    fits = frames == 1 and n % 2 == 0 and places % (16 * n) == 0 and limit + n <= 256 and n <= limit
+    fits = frames == 1 and n % 4 == 0 and places % (16 * n) == 0 and limit + n <= 256 and n <= limit
     return (kernel_body if fits else body)(latents, *rest)
 
 

time: 44 us -> 49 us (1.11)
  the two profiles are of different devices: /device:TPU:1 before, /device:TPU:3 now
where the time goes in v4:
time: 49 us; the launch traced here: 48.9 us
  Pallas kernels  47.2 us (96%)
  local copies, waits for them, and re-layouts  1.73 us (4%)
    pallas_call x1, Pallas kernels, kernel_body(): pl.pallas_call(functools.partial(block_kernel, n, share), out_shape=jax.S...  47.2 us
    unnamed x1, local copies, waits for them, and re-layouts  1.73 us

profile of v4, /device:TPU:3, one launch (start us, length us, event | category | flops | bytes accessed | tf_op | source)
XLA Modules:
  0.0 48.9 jit_solution(10173141785037679716)
XLA Ops:
  0.0 47.2 %shard_map.109 = bf16[1,256,640]{2,1,0:T(8,128)(2,1)} custom-call(bf16[1,256,640]{2,1,0:T(8,128)(2,1)} %lat.1, bf16[640,640]{1,0:T(8,128)(2,1)} %refs_0_.1, bf16[640,640]{1,0:T(8,128)(2,1)} %refs_1_.1, bf16[640,640]{1,0:T(8,128)(2,1)} %refs_2_.1, bf16[640,640]{1,0:T(8,128)(2,1)} %refs_3_.1, bf16[640,640]{1,0:T(8,128)(2,1)} %refs_4_.1, ...), custom_call_target="tpu_custom_call" | custom-call | tf_op jit(solution)/shard_map/pallas_call | solution.py:559
  47.2 1.7 %copy.13 = bf16[1,256,640]{2,1,0:T(8,128)(2,1)} copy(bf16[1,256,640]{2,1,0:T(8,128)(2,1)} %shard_map.109) | data formatting | bytes 655360

commit v5 on v3

--- a/solution.py
+++ b/solution.py
@@ -175,7 +175,7 @@
     return spans
 
 
-def attend(q_ref, k_ref, v_ref, rows, scale, bias_ref):
+def attend(q_ref, k_ref, v_ref, rows, scale, bias_ref, acc=None, stat=None):
     channels = q_ref.shape[-1]
     tiles = [None] * (channels // LANES)
     for head, (low, high, begin, end) in enumerate(windows(channels)):
@@ -187,7 +187,8 @@
             query, k_ref[:, low:high], (((1,), (1,)), ((), ())), preferred_element_type=jnp.float32
         )
         if bias_ref is None:
-            highest = jnp.max(scores, axis=-1, keepdims=True)
+            before = stat[head, rows, 0:1]
+            highest = jnp.maximum(jnp.max(scores, axis=-1, keepdims=True), before)
             powered = jnp.exp2((scores - highest) * (scale * LOG2E))
         else:
             scores = scores * scale + bias_ref[head, rows, :]
@@ -197,6 +198,10 @@
         mixed = jnp.dot(
             powered.astype(jnp.bfloat16), v_ref[:, low:high], preferred_element_type=jnp.float32
         )
+        if bias_ref is None:
+            fade = jnp.exp2((before - highest) * (scale * LOG2E))
+            total = total + stat[head, rows, 1:2] * fade
+            mixed = mixed + acc[head, rows, : high - low] * fade
         mixed = mixed * (1.0 / total)
         for at in range(low, high, LANES):
             part = mixed[:, at - low : at - low + LANES]
@@ -204,6 +209,23 @@
             old = tiles[at // LANES]
             tiles[at // LANES] = part if old is None else jnp.where(keep, part, old)
     return jnp.concatenate([t.astype(jnp.bfloat16) for t in tiles], axis=1)
+
+
+def attend_prior(q_ref, k_ref, v_ref, rows, scale, acc, stat):
+    for head, (low, high, begin, end) in enumerate(windows(q_ref.shape[-1])):
+        lane = lax.broadcasted_iota(jnp.int32, (rows.size, high - low), 1)
+        query = q_ref[rows, low:high]
+        query = jnp.where((lane >= begin) & (lane < end), query, jnp.zeros_like(query))
+        scores = lax.dot_general(
+            query, k_ref[:, low:high], (((1,), (1,)), ((), ())), preferred_element_type=jnp.float32
+        )
+        highest = jnp.max(scores, axis=-1, keepdims=True)
+        powered = jnp.exp2((scores - highest) * (scale * LOG2E))
+        stat[head, rows, 0:1] = highest
+        stat[head, rows, 1:2] = jnp.sum(powered, axis=-1, keepdims=True)
+        acc[head, rows, : high - low] = jnp.dot(
+            powered.astype(jnp.bfloat16), v_ref[:, low:high], preferred_element_type=jnp.float32
+        )
 
 
 def norm_rows(floats):
@@ -239,6 +261,8 @@
         back_go,
         back_came,
         bias,
+        acc,
+        stat,
         pos_bias,
         buckets,
         x_sem,
@@ -371,6 +395,15 @@
     k[places:, :] = matmul(normed, w[1]).astype(jnp.bfloat16)
     v[places:, :] = matmul(normed, w[2]).astype(jnp.bfloat16)
 
+    halves = 2
+    size = places // halves
+
+    def prior_block(half):
+        rows = pl.ds(pl.multiple_of(half * size, size), size)
+        attend_prior(q, k.at[places:], v.at[places:], rows, scale, acc, stat)
+
+    pl.loop(0, halves)(prior_block)
+
     @pl.when(me > 0)
     def _():
         @pl.loop(0, n // 2)
@@ -383,9 +416,6 @@
 
     for i in range(3, 8):
         loads[i].wait()
-
-    halves = 2
-    size = places // halves
 
     def place(device):
         return lax.rem(device, 2) * (n // 2) + device // 2
@@ -418,7 +448,7 @@
 
     def space_block(half):
         rows = pl.ds(pl.multiple_of(half * size, size), size)
-        mix = attend(q, k, v, rows, scale, None)
+        mix = attend(q, k.at[:places], v.at[:places], rows, scale, None, acc, stat)
         summed = x[rows, :].astype(jnp.float32) + matmul(mix, w[3])
         rounded = summed.astype(jnp.bfloat16)
         after[rows, :] = rounded
@@ -574,6 +604,8 @@
             blocks,
             blocks,
             pltpu.VMEM((HEADS, rows, rows), jnp.float32),
+            pltpu.VMEM((HEADS, places, 2 * LANES), jnp.float32),
+            pltpu.VMEM((HEADS, places, LANES), jnp.float32),
             pltpu.VMEM(position_bias.shape, jnp.float32),
             pltpu.VMEM(bucket_table.shape, jnp.int32),
             dma,

time: 44 us -> 47.2 us (1.073)
  Pallas kernels: 42.2 us -> 45.3 us
    pallas_call x1, Pallas kernels: 42.2 us -> 45.3 us  [kernel_body(): pl.pallas_call(functools.partial(block_kernel, n, share), out_shape=jax.S...]
where the time goes in v5:
time: 47.2 us; the launch traced here: 47 us
  Pallas kernels  45.3 us (96%)
  local copies, waits for them, and re-layouts  1.73 us (4%)
    pallas_call x1, Pallas kernels, kernel_body(): pl.pallas_call(functools.partial(block_kernel, n, share), out_shape=jax.S...  45.3 us
    unnamed x1, local copies, waits for them, and re-layouts  1.73 us

profile of v5, /device:TPU:1, one launch (start us, length us, event | category | flops | bytes accessed | tf_op | source)
XLA Modules:
  0.0 47.0 jit_solution(4361076303040241918)
XLA Ops:
  0.0 45.3 %shard_map.109 = bf16[1,256,640]{2,1,0:T(8,128)(2,1)} custom-call(bf16[1,256,640]{2,1,0:T(8,128)(2,1)} %lat.1, bf16[640,640]{1,0:T(8,128)(2,1)} %refs_0_.1, bf16[640,640]{1,0:T(8,128)(2,1)} %refs_1_.1, bf16[640,640]{1,0:T(8,128)(2,1)} %refs_2_.1, bf16[640,640]{1,0:T(8,128)(2,1)} %refs_3_.1, bf16[640,640]{1,0:T(8,128)(2,1)} %refs_4_.1, ...), custom_call_target="tpu_custom_call" | custom-call | tf_op jit(solution)/shard_map/pallas_call | solution.py:588
  45.3 1.7 %copy.13 = bf16[1,256,640]{2,1,0:T(8,128)(2,1)} copy(bf16[1,256,640]{2,1,0:T(8,128)(2,1)} %shard_map.109) | data formatting | bytes 655360

commit v6 on v3

--- a/solution.py
+++ b/solution.py
@@ -384,11 +384,11 @@
     for i in range(3, 8):
         loads[i].wait()
 
-    halves = 2
+    halves = 1
     size = places // halves
 
     def place(device):
-        return lax.rem(device, 2) * (n // 2) + device // 2
+        return device
 
     def to_owner(to):
         return pltpu.make_async_remote_copy(
@@ -410,7 +410,7 @@
 
         @pl.loop(0, count)
         def _(step):
-            to = 2 * lax.rem(me // 2 + step, count) + half
+            to = lax.rem(me + step, count)
 
             @pl.when(to != me)
             def _():
@@ -452,7 +452,7 @@
     same = lax.broadcasted_iota(jnp.int32, (share, n * share), 0) == lax.rem(
         lax.broadcasted_iota(jnp.int32, (share, n * share), 1), share
     )
-    order = list(range(0, n, 2)) + list(range(1, n, 2))
+    order = list(range(n))
     for block, i in enumerate(order):
         begin = (n - 1 - i) * share
         line = spread[:, begin : begin + n * share]

time: 44 us -> 44.4 us (level); the launches traced: 43.9 us -> 43.6 us
  no operation moved by 1% of the time
where the time goes in v6:
time: 44.4 us; the launch traced here: 43.6 us
  Pallas kernels  41.9 us (94%)
  local copies, waits for them, and re-layouts  1.73 us (4%)
    pallas_call x1, Pallas kernels, kernel_body(): pl.pallas_call(functools.partial(block_kernel, n, share), out_shape=jax.S...  41.9 us
    unnamed x1, local copies, waits for them, and re-layouts  1.73 us

profile of v6, /device:TPU:1, one launch (start us, length us, event | category | flops | bytes accessed | tf_op | source)
XLA Modules:
  0.0 43.6 jit_solution(4344926176104991110)
XLA Ops:
  0.0 41.9 %shard_map.109 = bf16[1,256,640]{2,1,0:T(8,128)(2,1)} custom-call(bf16[1,256,640]{2,1,0:T(8,128)(2,1)} %lat.1, bf16[640,640]{1,0:T(8,128)(2,1)} %refs_0_.1, bf16[640,640]{1,0:T(8,128)(2,1)} %refs_1_.1, bf16[640,640]{1,0:T(8,128)(2,1)} %refs_2_.1, bf16[640,640]{1,0:T(8,128)(2,1)} %refs_3_.1, bf16[640,640]{1,0:T(8,128)(2,1)} %refs_4_.1, ...), custom_call_target="tpu_custom_call" | custom-call | tf_op jit(solution)/shard_map/pallas_call | solution.py:558
  41.9 1.7 %copy.13 = bf16[1,256,640]{2,1,0:T(8,128)(2,1)} copy(bf16[1,256,640]{2,1,0:T(8,128)(2,1)} %shard_map.109) | data formatting | bytes 655360
